TPU v7x, 32 devices: a whole 2x2x4 slice. The times are simulated.
32 devices in a mesh: sa: 8 (over y, x, core), tp: 4 (over z).
Axes of the slice: x: 2, y: 2, z: 4, core: 2. Of those that a mesh axis runs over, the one named last changes fastest.
Arguments:
- window: float32 [2, 2, 16, 32, 512], P(None, None, 'sa', None, 'tp'), may hold values from -4 to 4
- damping: float32 [16, 32], P('sa'), may hold values from 0 to 1
- propagator: float32 [2, 32, 32], replicated, may hold values from -1 to 1, as said below
- coupling: float32 [32], replicated, may hold values from 0.5 to 1.5
Outputs:
- lesser_next: float32 [2, 16, 32, 512], P(None, 'sa', None, 'tp')
Inputs may be any that keep to these rules, and one draw needn't show every extreme that they name: `propagator`: a unitary matrix.
All inputs are finite; a program needn't handle non-finite values.
Results may differ from a plain program's by a relative error of at most 0.0079.
Values may be sent and summed in bfloat16 or wider, within the bound.
A program may use at most 64 MiB of HBM per device.

v0:
```python
import math

import jax
import jax.numpy as jnp
from jax import lax
from jax.sharding import PartitionSpec as P

highest = lax.Precision.HIGHEST


def prefix_2(value, axis, join, neutral):
    count, mine = (lax.axis_size(axis), lax.axis_index(axis))
    pieces = jax.tree.map(lambda part: lax.all_gather(part, axis), value)
    running = jax.tree.map(
        lambda part, zero: jnp.full_like(part, 0) + jnp.asarray(zero, part.dtype), value, neutral
    )

    def lap(position, running):
        longer = join(running, jax.tree.map(lambda part: part[position], pieces))
        return jax.tree.map(lambda new, old: jnp.where(position < mine, new, old), longer, running)

    return lax.fori_loop(0, count - 1, lap, running)


def spectral_self_energy(occupied_correlator, greater, coupling, column_tiles):
    factor = jnp.tile(coupling[:, None] * coupling[None, :], (1, column_tiles))
    less_re, less_im = (occupied_correlator[0], occupied_correlator[1])
    great_re, great_im = (greater[0], greater[1])
    lsquare_re = less_re * less_re - less_im * less_im
    lsquare_im = 2.0 * less_re * less_im
    gsquare_re = great_re * great_re - great_im * great_im
    gsquare_im = 2.0 * great_re * great_im
    sless_re = -factor * (lsquare_re * great_re + lsquare_im * great_im)
    sless_im = -factor * (lsquare_im * great_re - lsquare_re * great_im)
    sgreat_re = -factor * (gsquare_re * less_re + gsquare_im * less_im)
    sgreat_im = -factor * (gsquare_im * less_re - gsquare_re * less_im)
    return jnp.stack([sgreat_re - sless_re, sgreat_im - sless_im]).astype(jnp.bfloat16)


def complex_product(left_re, left_im, right_re, right_im):
    cosine_component = jnp.dot(left_re, right_re, precision=highest) - jnp.dot(
        left_im, right_im, precision=highest
    )
    imag_part = jnp.dot(left_re, right_im, precision=highest) + jnp.dot(
        left_im, right_re, precision=highest
    )
    return (cosine_component, imag_part)


def propagate(forcing, damping, propagator, initial):

    def advance(state, inputs):
        damp_row, force_row = inputs
        cosine_component, imag_part = complex_product(
            propagator[0], propagator[1], state[0], state[1]
        )
        advanced = damp_row[None, :, None] * jnp.stack([cosine_component, imag_part]) + force_row
        return (advanced, advanced)

    last_state, produced = lax.scan(advance, initial, (damping, jnp.moveaxis(forcing, 1, 0)))
    return jnp.moveaxis(produced, 0, 1)


def combine(earlier, following):
    carry_re, carry_im = complex_product(following[0], following[1], earlier[0], earlier[1])
    shift_re, shift_im = complex_product(following[0], following[1], earlier[2], earlier[3])
    return (carry_re, carry_im, shift_re + following[2], shift_im + following[3])


def shards(window, damping, propagator, coupling):
    occupied_correlator = window[0]
    greater = window[1]
    orbitals = coupling.shape[0]
    block_rows = occupied_correlator.shape[1]
    column_entries = occupied_correlator.shape[3]
    column_tiles = column_entries // orbitals
    horizon = block_rows * lax.axis_size("sa")
    weight_scale = 1.0 / (horizon * math.sqrt(orbitals))
    position = lax.axis_index("sa")
    initial = occupied_correlator[:, 0]

    def collision(current):
        spectral = spectral_self_energy(current, greater, coupling, column_tiles)
        spectral_rows = lax.all_gather(spectral, "tp", axis=3, tiled=True)
        left_re = spectral_rows[0].reshape(block_rows * orbitals, -1)
        left_im = spectral_rows[1].reshape(block_rows * orbitals, -1)
        shard_piece = lax.all_gather(current.astype(jnp.bfloat16), "sa", axis=1, tiled=True)
        span_rows = shard_piece.shape[1] * orbitals
        piece_re = shard_piece[0].reshape(span_rows, column_entries)
        piece_im = shard_piece[1].reshape(span_rows, column_entries)
        cosine_component = jnp.dot(left_re, piece_re, preferred_element_type=jnp.float32) - jnp.dot(
            left_im, piece_im, preferred_element_type=jnp.float32
        )
        imag_part = jnp.dot(left_re, piece_im, preferred_element_type=jnp.float32) + jnp.dot(
            left_im, piece_re, preferred_element_type=jnp.float32
        )
        return weight_scale * jnp.stack([cosine_component, imag_part]).reshape(current.shape)

    def advance_block(forcing):
        start_state = jnp.where(position == 0, initial, jnp.zeros_like(initial))
        unit_real = jnp.eye(orbitals, dtype=jnp.float32)
        unit_imag = jnp.zeros((orbitals, orbitals), jnp.float32)
        resting = jnp.zeros((2, block_rows, orbitals, orbitals), jnp.float32)
        carried = propagate(resting, damping, propagator, jnp.stack([unit_real, unit_imag]))[:, -1]
        offset_rows = propagate(forcing, damping, propagator, start_state)[:, -1]
        active = jnp.where(position == 0, 0.0, 1.0)
        element = (active * carried[0], active * carried[1], offset_rows[0], offset_rows[1])
        blank = jnp.zeros((orbitals, column_entries), jnp.float32)
        identity = (unit_real, unit_imag, blank, blank)
        prefix = prefix_2(element, "sa", combine, identity)
        incoming = jnp.where(position == 0, initial, jnp.stack([prefix[2], prefix[3]]))
        return propagate(forcing, damping, propagator, incoming)

    first_term = collision(occupied_correlator)
    predicted = advance_block(first_term)
    second_term = collision(predicted)
    return advance_block(0.5 * (first_term + second_term))


def solution(mesh):
    return jax.shard_map(
        shards,
        mesh=mesh,
        in_specs=(P(None, None, "sa", None, "tp"), P("sa", None), P(), P()),
        out_specs=P(None, "sa", None, "tp"),
        check_vma=False,
    )
```

profile of v0, /device:TPU:0, one launch (start us, length us, event | category | flops | bytes accessed | tf_op | source)
XLA Modules:
  0.0 118.8 jit_solution(4401782386184903191)
XLA Ops:
  0.0 0.8 multiply_negate_fusion
  1.0 14.0 %all_gather.38 = bf16[2,2,32,512]{3,2,0,1:T(8,128)(2,1)S(1)} all-gather(bf16[2,2,32,128]{3,2,0,1:T(8,128)(2,1)S(1)} %pad_maximum_fusion), channel_id=1, replica_groups=mesh['sa'=8,'tp'=4] {'tp'}, dimensions={3}, use_global_device_ids=true | all-gather | bytes 163840 | tf_op jit(solution)/shard_map/all_gather | solution.py:84
  15.0 9.3 %all_gather.39 = bf16[2,16,32,128]{3,2,0,1:T(8,128)(2,1)S(1)} all-gather(bf16[2,2,32,128]{3,2,0,1:T(8,128)(2,1)S(1)} %fusion.207), channel_id=1, replica_groups=mesh['sa'=8,'tp'=4] {'sa'}, dimensions={1}, use_global_device_ids=true | all-gather | bytes 294912 | tf_op jit(solution)/shard_map/all_gather | solution.py:87
  24.5 0.2 convolution_subtract_fusion.8
  25.0 0.6 copy-done.1
  25.7 0.7 copy-done
  26.4 1.5 %while.98 = (s32[]{:T(128)}, f32[2,32,128]{2,1,0:T(8,128)S(1)}, f32[2,2,32,128]{3,2,0,1:T(8,128)S(1)}, f32[2,32]{1,0:T(2,128)S(1)}, f32[2,32,32]{2,1,0:T(8,128)S(1)}, /*index=5*/f32[2,2,32,128]{3,2,1,0:T(8,128)S(1)}, s32[]{:T(128)}) while((s32[]{:T(128)}, f32[2,32,128]{2,1,0:T(8,128)S(1)}, f32[2,2,32,128]{3,2,0,1:T(8,128)S(1)}, ...), condition=%wide.region_3.4_spmd, body=%wide.region_2.3_spmd.sunk | while | flops 6348802 | bytes 426969 | solution.py:60
  27.9 9.2 %all-gather.2 = f32[8,1,32,128]{3,2,1,0:T(8,128)S(1)} all-gather(f32[1,1,32,128]{3,2,1,0:T(8,128)S(1)} %get-tuple-element.618), channel_id=4, replica_groups=mesh['sa'=8,'tp'=4] {'sa'}, dimensions={0}, use_global_device_ids=true | all-gather | bytes 147456 | tf_op jit(solution)/shard_map/all_gather | solution.py:13
  37.1 8.2 %all-gather.3 = f32[8,1,32,128]{3,2,1,0:T(8,128)S(1)} all-gather(f32[1,1,32,128]{3,2,1,0:T(8,128)S(1)} %get-tuple-element.617), channel_id=5, replica_groups=mesh['sa'=8,'tp'=4] {'sa'}, dimensions={0}, use_global_device_ids=true | all-gather | bytes 147456 | tf_op jit(solution)/shard_map/all_gather | solution.py:13
  45.4 1.5 %while.97 = (s32[]{:T(128)}, f32[2,32,32]{2,1,0:T(8,128)S(1)}, f32[2,2,32,32]{3,2,0,1:T(8,128)S(1)}, f32[2,32]{1,0:T(2,128)S(1)}, f32[2,32,32]{2,1,0:T(8,128)S(1)}, /*index=5*/s32[]{:T(128)}) while((s32[]{:T(128)}, f32[2,32,32]{2,1,0:T(8,128)S(1)}, f32[2,2,32,32]{3,2,0,1:T(8,128)S(1)}, f32[2,32]{1,0:T(2,128)S(1)}, f32[2,32,32]{2,1,0:T(8,128)S(1)}, ...), condition=%wide.region_1.2_spmd, body=%wide.region_0.1_spmd.sunk | while | flops 1583106 | bytes 263117 | solution.py:60
  46.9 9.2 %all-gather = f32[8,1,32,32]{3,2,1,0:T(8,128)S(1)} all-gather(f32[1,1,32,32]{3,2,1,0:T(8,128)S(1)} %get-tuple-element.620), channel_id=2, replica_groups=mesh['sa'=8,'tp'=4] {'sa'}, dimensions={0}, use_global_device_ids=true | all-gather | bytes 36864 | tf_op jit(solution)/shard_map/all_gather | solution.py:13
  56.1 8.2 %all-gather.1 = f32[8,1,32,32]{3,2,1,0:T(8,128)S(1)} all-gather(f32[1,1,32,32]{3,2,1,0:T(8,128)S(1)} %get-tuple-element.619), channel_id=3, replica_groups=mesh['sa'=8,'tp'=4] {'sa'}, dimensions={0}, use_global_device_ids=true | all-gather | bytes 36864 | tf_op jit(solution)/shard_map/all_gather | solution.py:13
  64.3 4.4 %while.102 = (s32[]{:T(128)}, f32[32,128]{1,0:T(8,128)S(1)}, f32[32,128]{1,0:T(8,128)S(1)}, s32[]{:T(128)}, f32[8,32,32]{2,1,0:T(8,128)S(1)}, /*index=5*/f32[8,3...) while((s32[]{:T(128)}, f32[32,128]{1,0:T(8,128)S(1)}, ...), condition=%wide.region_5.6_spmd.clone, body=%wide.region_4.5_spmd.clone.sunk | while | flops 6340612 | bytes 332929 | solution.py:22
  68.7 1.5 %while.99 = (s32[]{:T(128)}, f32[2,32,128]{2,1,0:T(8,128)S(1)}, f32[2,2,32,128]{3,2,1,0:T(8,128)S(1)}, f32[2,32]{1,0:T(2,128)S(1)}, f32[2,32,32]{2,1,0:T(8,128)S(1)}, /*index=5*/f32[2,2,32,128]{3,2,1,0:T(8,128)S(1)}, s32[]{:T(128)}) while((s32[]{:T(128)}, f32[2,32,128]{2,1,0:T(8,128)S(1)}, f32[2,2,32,128]{3,2,1,0:T(8,128)S(1)}, ...), condition=%wide.region_7.8_spmd, body=%wide.region_6.7_spmd.sunk | while | flops 6348802 | bytes 426969 | solution.py:60
  70.3 9.3 %all_gather.43 = bf16[2,16,32,128]{3,2,0,1:T(8,128)(2,1)S(1)} all-gather(bf16[2,2,32,128]{3,2,0,1:T(8,128)(2,1)S(1)} %bitcast_convert_fusion), channel_id=1, replica_groups=mesh['sa'=8,'tp'=4] {'sa'}, dimensions={1}, use_global_device_ids=true | all-gather | bytes 294912 | tf_op jit(solution)/shard_map/all_gather | solution.py:87
  79.6 12.3 %all_gather.42 = bf16[2,2,32,512]{3,2,0,1:T(8,128)(2,1)S(1)} all-gather(bf16[2,2,32,128]{3,2,0,1:T(8,128)(2,1)S(1)} %pad_maximum_fusion.1), channel_id=1, replica_groups=mesh['sa'=8,'tp'=4] {'tp'}, dimensions={3}, use_global_device_ids=true | all-gather | bytes 163840 | tf_op jit(solution)/shard_map/all_gather | solution.py:84
  92.4 0.2 convolution_add_fusion.7
  92.6 0.7 copy-done.2
  93.3 1.5 %while.100 = (s32[]{:T(128)}, f32[2,32,128]{2,1,0:T(8,128)S(1)}, f32[2,2,32,128]{3,2,0,1:T(8,128)S(1)}, f32[2,32]{1,0:T(2,128)S(1)}, f32[2,32,32]{2,1,0:T(8,128)S(1)}, /*index=5*/f32[2,2,32,128]{3,2,1,0:T(8,128)S(1)}, s32[]{:T(128)}) while((s32[]{:T(128)}, f32[2,32,128]{2,1,0:T(8,128)S(1)}, f32[2,2,32,128]{3,2,0,1:T(8,128)S(1)}, ...), condition=%wide.region_9.10_spmd, body=%wide.region_8.9_spmd.sunk | while | flops 6348802 | bytes 426969 | solution.py:60
  94.9 8.2 %all-gather.4 = f32[8,1,32,128]{3,2,1,0:T(8,128)S(1)} all-gather(f32[1,1,32,128]{3,2,1,0:T(8,128)S(1)} %get-tuple-element.616), channel_id=6, replica_groups=mesh['sa'=8,'tp'=4] {'sa'}, dimensions={0}, use_global_device_ids=true | all-gather | bytes 147456 | tf_op jit(solution)/shard_map/all_gather | solution.py:13
  103.1 9.2 %all-gather.5 = f32[8,1,32,128]{3,2,1,0:T(8,128)S(1)} all-gather(f32[1,1,32,128]{3,2,1,0:T(8,128)S(1)} %get-tuple-element.615), channel_id=7, replica_groups=mesh['sa'=8,'tp'=4] {'sa'}, dimensions={0}, use_global_device_ids=true | all-gather | bytes 147456 | tf_op jit(solution)/shard_map/all_gather | solution.py:13
  112.3 4.4 %while.103 = (s32[]{:T(128)}, f32[32,128]{1,0:T(8,128)S(1)}, f32[32,128]{1,0:T(8,128)S(1)}, s32[]{:T(128)}, f32[8,32,32]{2,1,0:T(8,128)S(1)}, /*index=5*/f32[8,3...) while((s32[]{:T(128)}, f32[32,128]{1,0:T(8,128)S(1)}, ...), condition=%wide.region_11.12_spmd.clone, body=%wide.region_10.11_spmd.clone.sunk | while | flops 6340612 | bytes 332929 | solution.py:22
  116.7 1.5 %while.101 = (s32[]{:T(128)}, f32[2,32,128]{2,1,0:T(8,128)S(1)}, f32[2,2,32,128]{3,2,0,1:T(8,128)S(1)}, f32[2,32]{1,0:T(2,128)S(1)}, f32[2,32,32]{2,1,0:T(8,128)S(1)}, /*index=5*/f32[2,2,32,128]{3,2,1,0:T(8,128)S(1)}, s32[]{:T(128)}) while((s32[]{:T(128)}, f32[2,32,128]{2,1,0:T(8,128)S(1)}, f32[2,2,32,128]{3,2,0,1:T(8,128)S(1)}, ...), condition=%wide.region_13.14_spmd, body=%wide.region_12.13_spmd.sunk | while | flops 6348802 | bytes 426969 | solution.py:60
  118.2 0.6 copy-done.5
  (188 shorter events, 17.0 us)
Async XLA Ops:
  0.0 0.9 copy-start.4
  25.0 0.6 copy-start.1
  25.0 0.7 copy-start.6
  25.6 0.8 copy-start
  25.6 0.8 copy-start.3
  92.6 0.8 copy-start.2
  118.2 0.6 copy-start.5
where the time goes:
time: 119 us
  blocking collectives  97 us (82%)
  matrix products  15.2 us (13%)
  local copies, waits for them, and re-layouts  3.1 us (3%)
  other arithmetic  2.49 us (2%)
    all_gather x6, blocking collectives, prefix_2(): pieces = jax.tree.map(lambda part: lax.all_gather(part, axis), value)  52.2 us
    all_gather x2, blocking collectives, collision(): spectral_rows = lax.all_gather(spectral, 'tp', axis=3, tiled=True)  26.2 us
    all_gather x2, blocking collectives, collision(): lax.all_gather(current.astype(jnp.bfloat16), 'sa', axis=1, tiled=True)  18.6 us
    dot_general x24, matrix products, complex_product(): jnp.dot(left_im, right_im, precision=highest)  3.76 us
    dot_general x24, matrix products, complex_product(): jnp.dot(left_im, right_re, precision=highest)  3.71 us
    dot_general x24, matrix products, complex_product(): jnp.dot(left_re, right_re, precision=highest)  3.25 us
    dot_general x24, matrix products, complex_product(): jnp.dot(left_re, right_im, precision=highest)  3.18 us
    unnamed x14, local copies, waits for them, and re-layouts  2.76 us

commit v1 on v0

v1 whole, which is shorter than its diff:
```python
import functools
import math

import jax
import jax.numpy as jnp
from jax import lax
from jax.experimental import pallas as pl
from jax.experimental.pallas import tpu as pltpu
from jax.sharding import PartitionSpec as P

MESH = pl.DeviceIdType.MESH
F32 = jnp.float32
BF16 = jnp.bfloat16


def exact(a, b):
    return jnp.dot(a, b, precision=lax.Precision.HIGHEST, preferred_element_type=F32)


def split(x):
    high = x.astype(BF16)
    return high, (x - high.astype(F32)).astype(BF16)


def mm(a, b):
    return jnp.dot(a, b, preferred_element_type=F32)


def mm3(a, b):
    return mm(a[0], b[0]) + (mm(a[0], b[1]) + mm(a[1], b[0]))


def spectral_of(x_re, x_im, g_re, g_im, factor):
    lsquare_re = x_re * x_re - x_im * x_im
    lsquare_im = 2.0 * x_re * x_im
    gsquare_re = g_re * g_re - g_im * g_im
    gsquare_im = 2.0 * g_re * g_im
    sless_re = -factor * (lsquare_re * g_re + lsquare_im * g_im)
    sless_im = -factor * (lsquare_im * g_re - lsquare_re * g_im)
    sgreat_re = -factor * (gsquare_re * x_re + gsquare_im * x_im)
    sgreat_im = -factor * (gsquare_im * x_re - gsquare_re * x_im)
    return jnp.concatenate([sgreat_re - sless_re, sgreat_im - sless_im], axis=0).astype(BF16)


def kernel(
    n_sa, n_tp, scale,
    win, damp, prop, coup, out,
    dall, hist, spec1, off, fev, hist2, spec2, off2, w_hi, w_lo,
    s_d, r_d, s_h, r_h, s_s1, r_s1, s_o, r_o, s_f, r_f, s_s2, r_s2, s_o2, r_o2,
):
    me_sa = lax.axis_index("sa")
    me_tp = lax.axis_index("tp")
    no = prop.shape[1]
    cols = win.shape[4]
    rows = win.shape[2] * no

    barrier = pltpu.get_barrier_semaphore()
    for k in range(1, n_sa):
        pl.semaphore_signal(
            barrier, inc=1, device_id=(lax.rem(me_sa + k, n_sa), me_tp), device_id_type=MESH
        )
    for k in range(1, n_tp):
        pl.semaphore_signal(
            barrier, inc=1, device_id=(me_sa, lax.rem(me_tp + k, n_tp)), device_id_type=MESH
        )

    def sa_copy(buf, send, recv, k):
        return pltpu.make_async_remote_copy(
            src_ref=buf.at[me_sa], dst_ref=buf.at[me_sa], send_sem=send.at[k - 1],
            recv_sem=recv.at[me_sa],
            device_id=(lax.rem(me_sa + k, n_sa), me_tp), device_id_type=MESH,
        )

    def sa_wait(buf, send, recv, k):
        who = lax.rem(me_sa + k, n_sa)
        pltpu.make_async_remote_copy(
            src_ref=buf.at[who], dst_ref=buf.at[who], send_sem=send.at[k - 1],
            recv_sem=recv.at[who], device_id=(who, me_tp), device_id_type=MESH,
        ).wait_recv()

    def tp_copy(buf, send, recv, k):
        return pltpu.make_async_remote_copy(
            src_ref=buf.at[me_tp], dst_ref=buf.at[me_tp], send_sem=send.at[k - 1],
            recv_sem=recv.at[me_tp],
            device_id=(me_sa, lax.rem(me_tp + k, n_tp)), device_id_type=MESH,
        )

    def tp_wait(buf, send, recv, k):
        who = lax.rem(me_tp + k, n_tp)
        pltpu.make_async_remote_copy(
            src_ref=buf.at[who], dst_ref=buf.at[who], send_sem=send.at[k - 1],
            recv_sem=recv.at[who], device_id=(me_sa, who), device_id_type=MESH,
        ).wait_recv()

    pending = []

    def send_sa(buf, send, recv):
        for k in range(1, n_sa):
            copy = sa_copy(buf, send, recv, k)
            copy.start()
            pending.append(copy)

    def send_tp(buf, send, recv):
        for k in range(1, n_tp):
            copy = tp_copy(buf, send, recv, k)
            copy.start()
            pending.append(copy)

    row_id = lax.broadcasted_iota(jnp.int32, (no, cols), 0)
    lane_id = lax.broadcasted_iota(jnp.int32, (no, cols), 1)
    tiled = (lax.rem(lane_id, no) == row_id).astype(F32)
    c_row = coup[...]
    c_lanes = exact(c_row, tiled)
    eye = lax.broadcasted_iota(jnp.int32, (no, no), 0) == lax.broadcasted_iota(jnp.int32, (no, no), 1)
    c_col = jnp.sum(jnp.where(eye, jnp.broadcast_to(c_row, (no, no)), 0.0), axis=1, keepdims=True)
    factor = c_col * c_lanes
    factor = jnp.concatenate([factor] * win.shape[2], axis=0)

    l_re = win[0, 0].reshape(rows, cols)
    l_im = win[0, 1].reshape(rows, cols)
    g_re = win[1, 0].reshape(rows, cols)
    g_im = win[1, 1].reshape(rows, cols)
    dmine = dall.at[me_sa]
    dmine[...] = jnp.zeros(dmine.shape, F32)
    dmine[0:2, 0:no] = damp[...]
    hmine = hist.at[me_sa]
    hmine[:, 0:cols] = l_re.astype(BF16)
    hmine[:, cols : 2 * cols] = l_im.astype(BF16)
    spec1[me_tp] = spectral_of(l_re, l_im, g_re, g_im, factor)

    pl.semaphore_wait(barrier, n_sa + n_tp - 2)
    send_tp(spec1, s_s1, r_s1)
    send_sa(dall, s_d, r_d)
    send_sa(hist, s_h, r_h)

    first = (lax.broadcasted_iota(jnp.int32, (no, 2 * no), 0)
             == lax.broadcasted_iota(jnp.int32, (no, 2 * no), 1)).astype(F32)
    second = (lax.broadcasted_iota(jnp.int32, (no, 2 * no), 0) + no
              == lax.broadcasted_iota(jnp.int32, (no, 2 * no), 1)).astype(F32)
    u_re, u_im = prop[0], prop[1]
    u_real = jnp.concatenate(
        [exact(u_re, first) - exact(u_im, second), exact(u_im, first) + exact(u_re, second)], axis=0
    )
    pick = (
        lax.rem(lax.broadcasted_iota(jnp.int32, (2 * no, 128), 0), no)
        == lax.broadcasted_iota(jnp.int32, (2 * no, 128), 1)
    )

    def scaled(d_row):
        wide = jnp.broadcast_to(d_row, (2 * no, 128))
        return jnp.sum(jnp.where(pick, wide, 0.0), axis=1, keepdims=True) * u_real

    def operators(ref):
        even = scaled(ref[0:1, :])
        odd = scaled(ref[1:2, :])
        both = exact(odd, even)
        return even, odd, both

    a_even, a_odd, b_mine = operators(dmine)
    a_odd_s = split(a_odd)
    m_mine = jnp.concatenate([a_even, b_mine], axis=0)
    x0 = jnp.concatenate([l_re[0:no], l_im[0:no]], axis=0)
    start = mm3(split(a_even), split(x0))
    start = jnp.where(me_sa == 0, start, jnp.zeros_like(start))

    for k in range(1, n_sa):
        sa_wait(dall, s_d, r_d, k)
    ops = []
    for q in range(n_sa):
        even, odd, both = operators(dall.at[q])
        ops.append(split(jnp.concatenate([even, both], axis=0)))
    current = jnp.zeros((4 * no, 2 * no), F32)
    for q in range(n_sa - 1, -1, -1):
        if q < n_sa - 1:
            nxt = ops[q + 1]
            current = mm3(split(current), (nxt[0][2 * no :], nxt[1][2 * no :]))
        current = jnp.where(me_sa == q + 1, m_mine, current)
        high, low = split(current)
        w_hi[q] = high
        w_lo[q] = low

    def forced(spec, history):
        acc = None
        for c in range(n_tp):
            part = mm(spec[c], history[c * cols : (c + 1) * cols, :])
            acc = part if acc is None else acc + part
        re = scale * (acc[0:rows, 0:cols] - acc[rows:, cols:])
        im = scale * (acc[0:rows, cols:] + acc[rows:, 0:cols])
        return (
            jnp.concatenate([re[0:no], im[0:no]], axis=0),
            jnp.concatenate([re[no:], im[no:]], axis=0),
        )

    def offsets(f_even, f_odd):
        f_even = f_even + start
        return f_even, mm3(a_odd_s, split(f_even)) + f_odd

    def own_rows(stack, f_even, offset):
        total = jnp.concatenate([f_even, offset], axis=0)
        for q in range(n_sa):
            block = stack[q]
            total = total + (mm(w_hi[q], block) + mm(w_lo[q], block))
        return total

    for k in range(1, n_sa):
        sa_wait(hist, s_h, r_h, k)
    for k in range(1, n_tp):
        tp_wait(spec1, s_s1, r_s1, k)
    f1_even, f1_odd = forced(spec1, hist[...].reshape(n_sa * rows, 2 * cols))
    fe, offset = offsets(f1_even, f1_odd)
    off[me_sa] = offset.astype(BF16)
    fev[me_sa] = fe.astype(BF16)
    send_sa(off, s_o, r_o)
    send_sa(fev, s_f, r_f)
    for k in range(1, n_sa):
        sa_wait(off, s_o, r_o, k)
    mine = own_rows(off, fe, offset)
    p_re = jnp.concatenate([mine[0:no], mine[2 * no : 3 * no]], axis=0)
    p_im = jnp.concatenate([mine[no : 2 * no], mine[3 * no :]], axis=0)
    spec2[me_tp] = spectral_of(p_re, p_im, g_re, g_im, factor)
    send_tp(spec2, s_s2, r_s2)

    for k in range(1, n_sa):
        sa_wait(fev, s_f, r_f, k)
    state = None
    for q in range(n_sa):
        x_even = fev[q].astype(F32)
        x_odd = off[q].astype(F32)
        if state is not None:
            moved = mm3(ops[q], split(state))
            x_even = x_even + moved[0 : 2 * no]
            x_odd = x_odd + moved[2 * no :]
        hist2[q, 0:no, 0:cols] = x_even[0:no].astype(BF16)
        hist2[q, 0:no, cols:] = x_even[no:].astype(BF16)
        hist2[q, no:, 0:cols] = x_odd[0:no].astype(BF16)
        hist2[q, no:, cols:] = x_odd[no:].astype(BF16)
        state = x_odd

    for k in range(1, n_tp):
        tp_wait(spec2, s_s2, r_s2, k)
    f2_even, f2_odd = forced(spec2, hist2[...].reshape(n_sa * rows, 2 * cols))
    fe2, offset2 = offsets(0.5 * (f1_even + f2_even), 0.5 * (f1_odd + f2_odd))
    off2[me_sa] = offset2.astype(BF16)
    send_sa(off2, s_o2, r_o2)
    for k in range(1, n_sa):
        sa_wait(off2, s_o2, r_o2, k)
    final = own_rows(off2, fe2, offset2)
    out[0, 0] = final[0:no]
    out[1, 0] = final[no : 2 * no]
    out[0, 1] = final[2 * no : 3 * no]
    out[1, 1] = final[3 * no :]
    for copy in pending:
        copy.wait_send()


def shards(window, damping, propagator, coupling):
    n_sa, n_tp = lax.axis_size("sa"), lax.axis_size("tp")
    no = coupling.shape[0]
    block = window.shape[2]
    cols = window.shape[4]
    rows = block * no
    scale = 1.0 / (block * n_sa * math.sqrt(no))
    dma = lambda n: pltpu.SemaphoreType.DMA((n,))
    vm = pl.BlockSpec(memory_space=pltpu.VMEM)
    pairs = []
    for n in (n_sa, n_sa, n_tp, n_sa, n_sa, n_tp, n_sa):
        pairs += [dma(n), dma(n)]
    return pl.pallas_call(
        functools.partial(kernel, n_sa, n_tp, scale),
        out_shape=jax.ShapeDtypeStruct((2, block, no, cols), F32),
        in_specs=[vm] * 4,
        out_specs=vm,
        scratch_shapes=[
            pltpu.VMEM((n_sa, 8, 128), F32),
            pltpu.VMEM((n_sa, rows, 2 * cols), BF16),
            pltpu.VMEM((n_tp, 2 * rows, cols), BF16),
            pltpu.VMEM((n_sa, 2 * no, cols), BF16),
            pltpu.VMEM((n_sa, 2 * no, cols), BF16),
            pltpu.VMEM((n_sa, rows, 2 * cols), BF16),
            pltpu.VMEM((n_tp, 2 * rows, cols), BF16),
            pltpu.VMEM((n_sa, 2 * no, cols), BF16),
            pltpu.VMEM((n_sa, 4 * no, 2 * no), BF16),
            pltpu.VMEM((n_sa, 4 * no, 2 * no), BF16),
        ] + pairs,
        compiler_params=pltpu.CompilerParams(collective_id=0, has_side_effects=True),
        name="kadanoff",
    )(window, damping, propagator, coupling.reshape(1, no))


def solution(mesh):
    return jax.shard_map(
        shards,
        mesh=mesh,
        in_specs=(P(None, None, "sa", None, "tp"), P("sa", None), P(), P()),
        out_specs=P(None, "sa", None, "tp"),
        check_vma=False,
    )
```

time: 119 us -> 27.9 us (0.23)
  blocking collectives: 97 us -> 0 us
  Pallas kernels: 0 us -> 26.2 us
  matrix products: 15.2 us -> 0 us
  other arithmetic: 2.49 us -> 0 us
  local copies, waits for them, and re-layouts: 3.1 us -> 1.47 us
    all_gather x10 -> x0, blocking collectives: 97 us -> none  [the longest x6 52.2 us: prefix_2(): pieces = jax.tree.map(lambda part: lax.all_gather(part, axis), value)]
    pallas_call x0 -> x1, Pallas kernels: none -> 26.2 us  [shards(): pl.pallas_call(functools.partial(kernel, n_sa, n_tp, scale), out_shape=ja...]
    dot_general x104 -> x0, matrix products: 15.2 us -> none  [the longest x24 3.76 us: complex_product(): jnp.dot(left_im, right_im, precision=highest)]
    unnamed x14 -> x1, local copies, waits for them, and re-layouts: 2.76 us -> 1.47 us
where the time goes in v1:
time: 27.9 us; the launch traced here: 27.7 us
  Pallas kernels  26.2 us (94%)
  local copies, waits for them, and re-layouts  1.47 us (5%)
    pallas_call x1, Pallas kernels, shards(): pl.pallas_call(functools.partial(kernel, n_sa, n_tp, scale), out_shape=ja...  26.2 us
    unnamed x1, local copies, waits for them, and re-layouts  1.47 us

profile of v1, /device:TPU:0, one launch (start us, length us, event | category | flops | bytes accessed | tf_op | source)
XLA Modules:
  0.0 27.7 jit_solution(18384375151237130654)
XLA Ops:
  0.0 26.2 %kadanoff.1 = f32[2,2,32,128]{3,2,1,0:T(8,128)} custom-call(f32[2,2,2,32,128]{4,3,2,1,0:T(8,128)} %win.1, f32[2,32]{1,0:T(2,128)} %damp.1, f32[2,32,32]{2,1,0:T(8,128)} %prop.1, f32[1,32]{1,0:T(1,128)} %bitcast.1), custom_call_target="tpu_custom_call" | custom-call | tf_op jit(solution)/shard_map/kadanoff/pallas_call | solution.py:268
  26.3 1.5 %copy.6 = f32[2,2,32,128]{3,2,1,0:T(8,128)} copy(f32[2,2,32,128]{3,2,1,0:T(8,128)} %kadanoff.1) | data formatting | bytes 131072

commit v2 on v1

--- a/solution.py
+++ b/solution.py
@@ -44,8 +44,8 @@
 
 def kernel(
     n_sa, n_tp, scale,
-    win, damp, prop, coup, out,
-    dall, hist, spec1, off, fev, hist2, spec2, off2, w_hi, w_lo,
+    win_in, damp_in, prop_in, coup_in, out,
+    win, damp, prop, coup, s_in, dall, hist, spec1, off, fev, hist2, spec2, off2, w_hi, w_lo,
     s_d, r_d, s_h, r_h, s_s1, r_s1, s_o, r_o, s_f, r_f, s_s2, r_s2, s_o2, r_o2,
 ):
     me_sa = lax.axis_index("sa")
@@ -64,6 +64,15 @@
             barrier, inc=1, device_id=(me_sa, lax.rem(me_tp + k, n_tp)), device_id_type=MESH
         )
 
+    loads = [
+        pltpu.make_async_copy(src, dst, s_in.at[n])
+        for n, (src, dst) in enumerate(
+            [(win_in, win), (coup_in, coup), (damp_in, damp), (prop_in, prop)]
+        )
+    ]
+    for load in loads:
+        load.start()
+
     def sa_copy(buf, send, recv, k):
         return pltpu.make_async_remote_copy(
             src_ref=buf.at[me_sa], dst_ref=buf.at[me_sa], send_sem=send.at[k - 1],
@@ -106,6 +115,8 @@
             copy.start()
             pending.append(copy)
 
+    for load in loads:
+        load.wait()
     row_id = lax.broadcasted_iota(jnp.int32, (no, cols), 0)
     lane_id = lax.broadcasted_iota(jnp.int32, (no, cols), 1)
     tiled = (lax.rem(lane_id, no) == row_id).astype(F32)
@@ -120,6 +131,7 @@
     l_im = win[0, 1].reshape(rows, cols)
     g_re = win[1, 0].reshape(rows, cols)
     g_im = win[1, 1].reshape(rows, cols)
+    off2[...] = jnp.zeros(off2.shape, BF16)
     dmine = dall.at[me_sa]
     dmine[...] = jnp.zeros(dmine.shape, F32)
     dmine[0:2, 0:no] = damp[...]
@@ -127,11 +139,6 @@
     hmine[:, 0:cols] = l_re.astype(BF16)
     hmine[:, cols : 2 * cols] = l_im.astype(BF16)
     spec1[me_tp] = spectral_of(l_re, l_im, g_re, g_im, factor)
-
-    pl.semaphore_wait(barrier, n_sa + n_tp - 2)
-    send_tp(spec1, s_s1, r_s1)
-    send_sa(dall, s_d, r_d)
-    send_sa(hist, s_h, r_h)
 
     first = (lax.broadcasted_iota(jnp.int32, (no, 2 * no), 0)
              == lax.broadcasted_iota(jnp.int32, (no, 2 * no), 1)).astype(F32)
@@ -163,6 +170,44 @@
     start = mm3(split(a_even), split(x0))
     start = jnp.where(me_sa == 0, start, jnp.zeros_like(start))
 
+    pl.semaphore_wait(barrier, n_sa + n_tp - 2)
+    send_tp(spec1, s_s1, r_s1)
+    send_sa(dall, s_d, r_d)
+    send_sa(hist, s_h, r_h)
+
+    def forced(spec, history):
+        acc = None
+        for c in range(n_tp):
+            part = mm(spec[c], history[c * cols : (c + 1) * cols, :])
+            acc = part if acc is None else acc + part
+        re = scale * (acc[0:rows, 0:cols] - acc[rows:, cols:])
+        im = scale * (acc[0:rows, cols:] + acc[rows:, 0:cols])
+        return (
+            jnp.concatenate([re[0:no], im[0:no]], axis=0),
+            jnp.concatenate([re[no:], im[no:]], axis=0),
+        )
+
+    def offsets(f_even, f_odd):
+        f_even = f_even + start
+        return f_even, mm3(a_odd_s, split(f_even)) + f_odd
+
+    def own_rows(stack, f_even, offset):
+        total = jnp.concatenate([f_even, offset], axis=0)
+        for q in range(n_sa):
+            block = stack[q]
+            total = total + (mm(w_hi[q], block) + mm(w_lo[q], block))
+        return total
+
+    for k in range(1, n_sa):
+        sa_wait(hist, s_h, r_h, k)
+    for k in range(1, n_tp):
+        tp_wait(spec1, s_s1, r_s1, k)
+    f1_even, f1_odd = forced(spec1, hist[...].reshape(n_sa * rows, 2 * cols))
+    fe, offset = offsets(f1_even, f1_odd)
+    off[me_sa] = offset.astype(BF16)
+    fev[me_sa] = fe.astype(BF16)
+    send_sa(off, s_o, r_o)
+    send_sa(fev, s_f, r_f)
     for k in range(1, n_sa):
         sa_wait(dall, s_d, r_d, k)
     ops = []
@@ -179,39 +224,6 @@
         w_hi[q] = high
         w_lo[q] = low
 
-    def forced(spec, history):
-        acc = None
-        for c in range(n_tp):
-            part = mm(spec[c], history[c * cols : (c + 1) * cols, :])
-            acc = part if acc is None else acc + part
-        re = scale * (acc[0:rows, 0:cols] - acc[rows:, cols:])
-        im = scale * (acc[0:rows, cols:] + acc[rows:, 0:cols])
-        return (
-            jnp.concatenate([re[0:no], im[0:no]], axis=0),
-            jnp.concatenate([re[no:], im[no:]], axis=0),
-        )
-
-    def offsets(f_even, f_odd):
-        f_even = f_even + start
-        return f_even, mm3(a_odd_s, split(f_even)) + f_odd
-
-    def own_rows(stack, f_even, offset):
-        total = jnp.concatenate([f_even, offset], axis=0)
-        for q in range(n_sa):
-            block = stack[q]
-            total = total + (mm(w_hi[q], block) + mm(w_lo[q], block))
-        return total
-
-    for k in range(1, n_sa):
-        sa_wait(hist, s_h, r_h, k)
-    for k in range(1, n_tp):
-        tp_wait(spec1, s_s1, r_s1, k)
-    f1_even, f1_odd = forced(spec1, hist[...].reshape(n_sa * rows, 2 * cols))
-    fe, offset = offsets(f1_even, f1_odd)
-    off[me_sa] = offset.astype(BF16)
-    fev[me_sa] = fe.astype(BF16)
-    send_sa(off, s_o, r_o)
-    send_sa(fev, s_f, r_f)
     for k in range(1, n_sa):
         sa_wait(off, s_o, r_o, k)
     mine = own_rows(off, fe, offset)
@@ -241,14 +253,29 @@
     f2_even, f2_odd = forced(spec2, hist2[...].reshape(n_sa * rows, 2 * cols))
     fe2, offset2 = offsets(0.5 * (f1_even + f2_even), 0.5 * (f1_odd + f2_odd))
     off2[me_sa] = offset2.astype(BF16)
-    send_sa(off2, s_o2, r_o2)
-    for k in range(1, n_sa):
-        sa_wait(off2, s_o2, r_o2, k)
+    for k in range(n_sa - 1, 0, -1):
+
+        @pl.when(me_sa + k < n_sa)
+        def _():
+            sa_copy(off2, s_o2, r_o2, k).start()
+
+    for k in range(1, n_sa):
+
+        @pl.when(me_sa - k >= 0)
+        def _():
+            sa_wait(off2, s_o2, r_o2, n_sa - k)
+
     final = own_rows(off2, fe2, offset2)
     out[0, 0] = final[0:no]
     out[1, 0] = final[no : 2 * no]
     out[0, 1] = final[2 * no : 3 * no]
     out[1, 1] = final[3 * no :]
+    for k in range(n_sa - 1, 0, -1):
+
+        @pl.when(me_sa + k < n_sa)
+        def _():
+            sa_copy(off2, s_o2, r_o2, k).wait_send()
+
     for copy in pending:
         copy.wait_send()
 
@@ -267,10 +294,15 @@
         pairs += [dma(n), dma(n)]
     return pl.pallas_call(
         functools.partial(kernel, n_sa, n_tp, scale),
-        out_shape=jax.ShapeDtypeStruct((2, block, no, cols), F32),
-        in_specs=[vm] * 4,
+        out_shape=pltpu.VMEM((2, block, no, cols), F32),
+        in_specs=[pl.BlockSpec(memory_space=pl.ANY)] * 4,
         out_specs=vm,
         scratch_shapes=[
+            pltpu.VMEM(window.shape, F32),
+            pltpu.VMEM(damping.shape, F32),
+            pltpu.VMEM(propagator.shape, F32),
+            pltpu.VMEM((1, no), F32),
+            dma(4),
             pltpu.VMEM((n_sa, 8, 128), F32),
             pltpu.VMEM((n_sa, rows, 2 * cols), BF16),
             pltpu.VMEM((n_tp, 2 * rows, cols), BF16),

time: 27.9 us -> 23.3 us (0.84)
  Pallas kernels: 26.2 us -> 22.5 us
  local copies, waits for them, and re-layouts: 1.47 us -> 0.63 us
    pallas_call x1, Pallas kernels: 26.2 us -> 22.5 us  [shards(): pl.pallas_call(functools.partial(kernel, n_sa, n_tp, scale), out_shape=pl...]
    unnamed x1, local copies, waits for them, and re-layouts: 1.47 us -> 0.63 us
where the time goes in v2:
time: 23.3 us; the launch traced here: 23.2 us
  Pallas kernels  22.5 us (97%)
  local copies, waits for them, and re-layouts  0.63 us (3%)
    pallas_call x1, Pallas kernels, shards(): pl.pallas_call(functools.partial(kernel, n_sa, n_tp, scale), out_shape=pl...  22.5 us
    unnamed x1, local copies, waits for them, and re-layouts  0.63 us

profile of v2, /device:TPU:0, one launch (start us, length us, event | category | flops | bytes accessed | tf_op | source)
XLA Modules:
  0.0 23.2 jit_solution(15393365419025278292)
XLA Ops:
  0.0 22.5 %kadanoff.1 = f32[2,2,32,128]{3,2,1,0:T(8,128)S(1)} custom-call(f32[2,2,2,32,128]{4,3,2,1,0:T(8,128)} %win_in.1, f32[2,32]{1,0:T(2,128)} %damp_in.1, f32[2,32,32]{2,1,0:T(8,128)} %prop_in.1, f32[1,32]{1,0:T(1,128)} %bitcast.1), custom_call_target="tpu_custom_call" | custom-call | tf_op jit(solution)/shard_map/kadanoff/pallas_call | solution.py:295
  22.6 0.6 %copy.6 = f32[2,2,32,128]{3,2,1,0:T(8,128)} copy(f32[2,2,32,128]{3,2,1,0:T(8,128)S(1)} %kadanoff.1) | data formatting | bytes 131072

commit v3 on v2

--- a/solution.py
+++ b/solution.py
@@ -45,7 +45,7 @@
 def kernel(
     n_sa, n_tp, scale,
     win_in, damp_in, prop_in, coup_in, out,
-    win, damp, prop, coup, s_in, dall, hist, spec1, off, fev, hist2, spec2, off2, w_hi, w_lo,
+    win, damp, prop, coup, s_in, dall, hist, spec1, off, hist2, spec2, off2, w_hi, w_lo,
     s_d, r_d, s_h, r_h, s_s1, r_s1, s_o, r_o, s_f, r_f, s_s2, r_s2, s_o2, r_o2,
 ):
     me_sa = lax.axis_index("sa")
@@ -117,6 +117,27 @@
 
     for load in loads:
         load.wait()
+    def send_later(buf, send, recv):
+        for k in range(n_sa - 1, 0, -1):
+
+            @pl.when(me_sa + k < n_sa)
+            def _():
+                sa_copy(buf, send, recv, k).start()
+
+    def drain_later(buf, send, recv):
+        for k in range(n_sa - 1, 0, -1):
+
+            @pl.when(me_sa + k < n_sa)
+            def _():
+                sa_copy(buf, send, recv, k).wait_send()
+
+    def wait_earlier(buf, send, recv):
+        for k in range(1, n_sa):
+
+            @pl.when(me_sa - k >= 0)
+            def _():
+                sa_wait(buf, send, recv, n_sa - k)
+
     row_id = lax.broadcasted_iota(jnp.int32, (no, cols), 0)
     lane_id = lax.broadcasted_iota(jnp.int32, (no, cols), 1)
     tiled = (lax.rem(lane_id, no) == row_id).astype(F32)
@@ -131,6 +152,7 @@
     l_im = win[0, 1].reshape(rows, cols)
     g_re = win[1, 0].reshape(rows, cols)
     g_im = win[1, 1].reshape(rows, cols)
+    off[...] = jnp.zeros(off.shape, BF16)
     off2[...] = jnp.zeros(off2.shape, BF16)
     dmine = dall.at[me_sa]
     dmine[...] = jnp.zeros(dmine.shape, F32)
@@ -205,77 +227,48 @@
     f1_even, f1_odd = forced(spec1, hist[...].reshape(n_sa * rows, 2 * cols))
     fe, offset = offsets(f1_even, f1_odd)
     off[me_sa] = offset.astype(BF16)
-    fev[me_sa] = fe.astype(BF16)
-    send_sa(off, s_o, r_o)
-    send_sa(fev, s_f, r_f)
+    send_later(off, s_o, r_o)
     for k in range(1, n_sa):
         sa_wait(dall, s_d, r_d, k)
     ops = []
     for q in range(n_sa):
-        even, odd, both = operators(dall.at[q])
-        ops.append(split(jnp.concatenate([even, both], axis=0)))
+        ops.append(split(operators(dall.at[q])[2]))
     current = jnp.zeros((4 * no, 2 * no), F32)
     for q in range(n_sa - 1, -1, -1):
         if q < n_sa - 1:
-            nxt = ops[q + 1]
-            current = mm3(split(current), (nxt[0][2 * no :], nxt[1][2 * no :]))
+            current = mm3(split(current), ops[q + 1])
         current = jnp.where(me_sa == q + 1, m_mine, current)
         high, low = split(current)
         w_hi[q] = high
         w_lo[q] = low
 
-    for k in range(1, n_sa):
-        sa_wait(off, s_o, r_o, k)
+    wait_earlier(off, s_o, r_o)
     mine = own_rows(off, fe, offset)
     p_re = jnp.concatenate([mine[0:no], mine[2 * no : 3 * no]], axis=0)
     p_im = jnp.concatenate([mine[no : 2 * no], mine[3 * no :]], axis=0)
     spec2[me_tp] = spectral_of(p_re, p_im, g_re, g_im, factor)
     send_tp(spec2, s_s2, r_s2)
 
+    h2mine = hist2.at[me_sa]
+    h2mine[:, 0:cols] = p_re.astype(BF16)
+    h2mine[:, cols:] = p_im.astype(BF16)
+    send_sa(hist2, s_f, r_f)
     for k in range(1, n_sa):
-        sa_wait(fev, s_f, r_f, k)
-    state = None
-    for q in range(n_sa):
-        x_even = fev[q].astype(F32)
-        x_odd = off[q].astype(F32)
-        if state is not None:
-            moved = mm3(ops[q], split(state))
-            x_even = x_even + moved[0 : 2 * no]
-            x_odd = x_odd + moved[2 * no :]
-        hist2[q, 0:no, 0:cols] = x_even[0:no].astype(BF16)
-        hist2[q, 0:no, cols:] = x_even[no:].astype(BF16)
-        hist2[q, no:, 0:cols] = x_odd[0:no].astype(BF16)
-        hist2[q, no:, cols:] = x_odd[no:].astype(BF16)
-        state = x_odd
-
+        sa_wait(hist2, s_f, r_f, k)
     for k in range(1, n_tp):
         tp_wait(spec2, s_s2, r_s2, k)
     f2_even, f2_odd = forced(spec2, hist2[...].reshape(n_sa * rows, 2 * cols))
     fe2, offset2 = offsets(0.5 * (f1_even + f2_even), 0.5 * (f1_odd + f2_odd))
     off2[me_sa] = offset2.astype(BF16)
-    for k in range(n_sa - 1, 0, -1):
-
-        @pl.when(me_sa + k < n_sa)
-        def _():
-            sa_copy(off2, s_o2, r_o2, k).start()
-
-    for k in range(1, n_sa):
-
-        @pl.when(me_sa - k >= 0)
-        def _():
-            sa_wait(off2, s_o2, r_o2, n_sa - k)
-
+    send_later(off2, s_o2, r_o2)
+    wait_earlier(off2, s_o2, r_o2)
     final = own_rows(off2, fe2, offset2)
     out[0, 0] = final[0:no]
     out[1, 0] = final[no : 2 * no]
     out[0, 1] = final[2 * no : 3 * no]
     out[1, 1] = final[3 * no :]
-    for k in range(n_sa - 1, 0, -1):
-
-        @pl.when(me_sa + k < n_sa)
-        def _():
-            sa_copy(off2, s_o2, r_o2, k).wait_send()
-
+    drain_later(off, s_o, r_o)
+    drain_later(off2, s_o2, r_o2)
     for copy in pending:
         copy.wait_send()
 
@@ -307,7 +300,6 @@
             pltpu.VMEM((n_sa, rows, 2 * cols), BF16),
             pltpu.VMEM((n_tp, 2 * rows, cols), BF16),
             pltpu.VMEM((n_sa, 2 * no, cols), BF16),
-            pltpu.VMEM((n_sa, 2 * no, cols), BF16),
             pltpu.VMEM((n_sa, rows, 2 * cols), BF16),
             pltpu.VMEM((n_tp, 2 * rows, cols), BF16),
             pltpu.VMEM((n_sa, 2 * no, cols), BF16),

time: 23.3 us -> 22.8 us (0.979); the launches traced: 23.2 us -> 22.4 us
  Pallas kernels: 22.5 us -> 21.7 us
    pallas_call x1, Pallas kernels: 22.5 us -> 21.7 us  [shards(): pl.pallas_call(functools.partial(kernel, n_sa, n_tp, scale), out_shape=pl...]
where the time goes in v3:
time: 22.8 us; the launch traced here: 22.4 us
  Pallas kernels  21.7 us (95%)
  local copies, waits for them, and re-layouts  0.63 us (3%)
    pallas_call x1, Pallas kernels, shards(): pl.pallas_call(functools.partial(kernel, n_sa, n_tp, scale), out_shape=pl...  21.7 us
    unnamed x1, local copies, waits for them, and re-layouts  0.63 us

profile of v3, /device:TPU:0, one launch (start us, length us, event | category | flops | bytes accessed | tf_op | source)
XLA Modules:
  0.0 22.4 jit_solution(7798052030576139820)
XLA Ops:
  0.0 21.7 %kadanoff.1 = f32[2,2,32,128]{3,2,1,0:T(8,128)S(1)} custom-call(f32[2,2,2,32,128]{4,3,2,1,0:T(8,128)} %win_in.1, f32[2,32]{1,0:T(2,128)} %damp_in.1, f32[2,32,32]{2,1,0:T(8,128)} %prop_in.1, f32[1,32]{1,0:T(1,128)} %bitcast.1), custom_call_target="tpu_custom_call" | custom-call | tf_op jit(solution)/shard_map/kadanoff/pallas_call | solution.py:288
  21.8 0.6 %copy.6 = f32[2,2,32,128]{3,2,1,0:T(8,128)} copy(f32[2,2,32,128]{3,2,1,0:T(8,128)S(1)} %kadanoff.1) | data formatting | bytes 131072

commit v4 on v3

--- a/solution.py
+++ b/solution.py
@@ -45,7 +45,7 @@
 def kernel(
     n_sa, n_tp, scale,
     win_in, damp_in, prop_in, coup_in, out,
-    win, damp, prop, coup, s_in, dall, hist, spec1, off, hist2, spec2, off2, w_hi, w_lo,
+    win, damp, prop, coup, s_in, dall, hist, spec1, off, back, even2, hist2, spec2, off2, w_hi, w_lo,
     s_d, r_d, s_h, r_h, s_s1, r_s1, s_o, r_o, s_f, r_f, s_s2, r_s2, s_o2, r_o2,
 ):
     me_sa = lax.axis_index("sa")
@@ -117,6 +117,13 @@
 
     for load in loads:
         load.wait()
+    def back_copy(k):
+        return pltpu.make_async_remote_copy(
+            src_ref=off.at[me_sa], dst_ref=back.at[me_sa], send_sem=s_o.at[k - 1],
+            recv_sem=r_o.at[me_sa],
+            device_id=(lax.rem(me_sa + k, n_sa), me_tp), device_id_type=MESH,
+        )
+
     def send_later(buf, send, recv):
         for k in range(n_sa - 1, 0, -1):
 
@@ -153,6 +160,7 @@
     g_re = win[1, 0].reshape(rows, cols)
     g_im = win[1, 1].reshape(rows, cols)
     off[...] = jnp.zeros(off.shape, BF16)
+    back[...] = jnp.zeros(back.shape, BF16)
     off2[...] = jnp.zeros(off2.shape, BF16)
     dmine = dall.at[me_sa]
     dmine[...] = jnp.zeros(dmine.shape, F32)
@@ -229,6 +237,12 @@
     off[me_sa] = offset.astype(BF16)
     send_later(off, s_o, r_o)
     for k in range(1, n_sa):
+
+        @pl.when(me_sa + k >= n_sa)
+        def _():
+            back_copy(k).start()
+
+    for k in range(1, n_sa):
         sa_wait(dall, s_d, r_d, k)
     ops = []
     for q in range(n_sa):
@@ -249,12 +263,24 @@
     spec2[me_tp] = spectral_of(p_re, p_im, g_re, g_im, factor)
     send_tp(spec2, s_s2, r_s2)
 
-    h2mine = hist2.at[me_sa]
-    h2mine[:, 0:cols] = p_re.astype(BF16)
-    h2mine[:, cols:] = p_im.astype(BF16)
-    send_sa(hist2, s_f, r_f)
-    for k in range(1, n_sa):
-        sa_wait(hist2, s_f, r_f, k)
+    even2[me_sa, :, 0:cols] = p_re[0:no].astype(BF16)
+    even2[me_sa, :, cols:] = p_im[0:no].astype(BF16)
+    send_sa(even2, s_f, r_f)
+    for k in range(1, n_sa):
+
+        @pl.when(me_sa + k < n_sa)
+        def _():
+            sa_wait(back, s_o, r_o, k)
+
+    state = None
+    for q in range(n_sa):
+        block = off[q].astype(F32) + back[q].astype(F32)
+        state = block if state is None else mm3(ops[q], split(state)) + block
+        hist2[q, no:, 0:cols] = state[0:no].astype(BF16)
+        hist2[q, no:, cols:] = state[no:].astype(BF16)
+    for k in range(1, n_sa):
+        sa_wait(even2, s_f, r_f, k)
+    hist2[:, 0:no, :] = even2[...]
     for k in range(1, n_tp):
         tp_wait(spec2, s_s2, r_s2, k)
     f2_even, f2_odd = forced(spec2, hist2[...].reshape(n_sa * rows, 2 * cols))
@@ -268,6 +294,12 @@
     out[0, 1] = final[2 * no : 3 * no]
     out[1, 1] = final[3 * no :]
     drain_later(off, s_o, r_o)
+    for k in range(1, n_sa):
+
+        @pl.when(me_sa + k >= n_sa)
+        def _():
+            back_copy(k).wait_send()
+
     drain_later(off2, s_o2, r_o2)
     for copy in pending:
         copy.wait_send()
@@ -300,6 +332,8 @@
             pltpu.VMEM((n_sa, rows, 2 * cols), BF16),
             pltpu.VMEM((n_tp, 2 * rows, cols), BF16),
             pltpu.VMEM((n_sa, 2 * no, cols), BF16),
+            pltpu.VMEM((n_sa, 2 * no, cols), BF16),
+            pltpu.VMEM((n_sa, no, 2 * cols), BF16),
             pltpu.VMEM((n_sa, rows, 2 * cols), BF16),
             pltpu.VMEM((n_tp, 2 * rows, cols), BF16),
             pltpu.VMEM((n_sa, 2 * no, cols), BF16),

time: 22.8 us -> 22.2 us (0.974)
  the two profiles are of different devices: /device:TPU:0 before, /device:TPU:4 now
where the time goes in v4:
time: 22.2 us; the launch traced here: 22.1 us
  Pallas kernels  21.4 us (96%)
  local copies, waits for them, and re-layouts  0.63 us (3%)
    pallas_call x1, Pallas kernels, shards(): pl.pallas_call(functools.partial(kernel, n_sa, n_tp, scale), out_shape=pl...  21.4 us
    unnamed x1, local copies, waits for them, and re-layouts  0.63 us

profile of v4, /device:TPU:4, one launch (start us, length us, event | category | flops | bytes accessed | tf_op | source)
XLA Modules:
  0.0 22.1 jit_solution(8405531776278760233)
XLA Ops:
  0.0 21.4 %kadanoff.1 = f32[2,2,32,128]{3,2,1,0:T(8,128)S(1)} custom-call(f32[2,2,2,32,128]{4,3,2,1,0:T(8,128)} %win_in.1, f32[2,32]{1,0:T(2,128)} %damp_in.1, f32[2,32,32]{2,1,0:T(8,128)} %prop_in.1, f32[1,32]{1,0:T(1,128)} %bitcast.1), custom_call_target="tpu_custom_call" | custom-call | tf_op jit(solution)/shard_map/kadanoff/pallas_call | solution.py:320
  21.5 0.6 %copy.6 = f32[2,2,32,128]{3,2,1,0:T(8,128)} copy(f32[2,2,32,128]{3,2,1,0:T(8,128)S(1)} %kadanoff.1) | data formatting | bytes 131072

commit v5 on v4

--- a/solution.py
+++ b/solution.py
@@ -223,10 +223,8 @@
 
     def own_rows(stack, f_even, offset):
         total = jnp.concatenate([f_even, offset], axis=0)
-        for q in range(n_sa):
-            block = stack[q]
-            total = total + (mm(w_hi[q], block) + mm(w_lo[q], block))
-        return total
+        flat = stack[...].reshape(n_sa * 2 * no, cols)
+        return total + (mm(w_hi[...], flat) + mm(w_lo[...], flat))
 
     for k in range(1, n_sa):
         sa_wait(hist, s_h, r_h, k)
@@ -253,8 +251,8 @@
             current = mm3(split(current), ops[q + 1])
         current = jnp.where(me_sa == q + 1, m_mine, current)
         high, low = split(current)
-        w_hi[q] = high
-        w_lo[q] = low
+        w_hi[:, 2 * no * q : 2 * no * (q + 1)] = high
+        w_lo[:, 2 * no * q : 2 * no * (q + 1)] = low
 
     wait_earlier(off, s_o, r_o)
     mine = own_rows(off, fe, offset)
@@ -337,8 +335,8 @@
             pltpu.VMEM((n_sa, rows, 2 * cols), BF16),
             pltpu.VMEM((n_tp, 2 * rows, cols), BF16),
             pltpu.VMEM((n_sa, 2 * no, cols), BF16),
-            pltpu.VMEM((n_sa, 4 * no, 2 * no), BF16),
-            pltpu.VMEM((n_sa, 4 * no, 2 * no), BF16),
+            pltpu.VMEM((4 * no, n_sa * 2 * no), BF16),
+            pltpu.VMEM((4 * no, n_sa * 2 * no), BF16),
         ] + pairs,
         compiler_params=pltpu.CompilerParams(collective_id=0, has_side_effects=True),
         name="kadanoff",

time: 22.2 us -> 21.9 us (0.986)
  the two profiles are of different devices: /device:TPU:4 before, /device:TPU:0 now
where the time goes in v5:
time: 21.9 us; the launch traced here: 21.5 us
  Pallas kernels  20.9 us (95%)
  local copies, waits for them, and re-layouts  0.63 us (3%)
    pallas_call x1, Pallas kernels, shards(): pl.pallas_call(functools.partial(kernel, n_sa, n_tp, scale), out_shape=pl...  20.9 us
    unnamed x1, local copies, waits for them, and re-layouts  0.63 us

profile of v5, /device:TPU:0, one launch (start us, length us, event | category | flops | bytes accessed | tf_op | source)
XLA Modules:
  0.0 21.5 jit_solution(7290536110275673490)
XLA Ops:
  0.0 20.9 %kadanoff.1 = f32[2,2,32,128]{3,2,1,0:T(8,128)S(1)} custom-call(f32[2,2,2,32,128]{4,3,2,1,0:T(8,128)} %win_in.1, f32[2,32]{1,0:T(2,128)} %damp_in.1, f32[2,32,32]{2,1,0:T(8,128)} %prop_in.1, f32[1,32]{1,0:T(1,128)} %bitcast.1), custom_call_target="tpu_custom_call" | custom-call | tf_op jit(solution)/shard_map/kadanoff/pallas_call | solution.py:318
  20.9 0.6 %copy.6 = f32[2,2,32,128]{3,2,1,0:T(8,128)} copy(f32[2,2,32,128]{3,2,1,0:T(8,128)S(1)} %kadanoff.1) | data formatting | bytes 131072
